TPU v7x, 32 devices: a whole 2x2x4 slice. The times are simulated.
32 devices in a mesh: tm: 8 (over z, y), tensor: 4 (over x, core).
Axes of the slice: x: 2, y: 2, z: 4, core: 2. Of those that a mesh axis runs over, the one named last changes fastest.
Arguments:
- frames_in: bfloat16 [8, 1024, 768], P('tm'), may hold values from -16 to 16
- norm_gain: float32 [768], replicated, may hold values from 0.1 to 1.9
- w_qkv: bfloat16 [768, 3, 768], P(None, None, 'tensor'), may hold values from -0.21650635 to 0.21650635
- w_out: bfloat16 [768, 768], P('tensor'), may hold values from -0.21875 to 0.21875
- keep_runs: int32 [8, 16, 2], replicated, may hold values from 0 to 1023, as said below
- out_cotangent: bfloat16 [8, 1024, 768], P('tm'), may hold values from -6 to 6
Outputs:
- block_out: bfloat16 [8, 1024, 768], P('tm', None, 'tensor')
- grad_in: bfloat16 [8, 1024, 768], P('tm', None, 'tensor')
- grad_qkv: bfloat16 [768, 3, 768], P('tm', None, 'tensor')
- grad_proj: bfloat16 [768, 768], P('tensor', 'tm')
- grad_gain: float32 [768], P('tensor')
Inputs may be any that keep to these rules, and one draw needn't show every extreme that they name: keep_runs[t, r] = (first, length) is the r-th run of kept positions of frame t; the 16 runs of a frame are disjoint, in rising order, and lie within the frame's 1024 positions.
All inputs are finite; a program needn't handle non-finite values.
Results may differ from a plain program's by a relative error of at most 0.034.
Values may be sent and summed in bfloat16 or wider, within the bound.
No kernel may reach another device: no remote copies, remote signals or barrier semaphores. Data moves between devices by JAX's collectives and lax.ppermute only.
A program may use at most 128 MiB of HBM per device.

v0:
```python
import jax
import jax.numpy as jnp
from jax import lax
from jax.sharding import PartitionSpec as P

D = 768
H = 12
epsilon = 1e-05


def kept_table(keep_runs, first_place, place_count):
    places = first_place + jnp.arange(place_count, dtype=jnp.int32)
    starts = keep_runs[:, :, 0:1]
    lengths = keep_runs[:, :, 1:2]
    inside = (places[None, None, :] >= starts) & (places[None, None, :] < starts + lengths)
    return jnp.sum(inside.astype(jnp.int32), axis=1)


def normalize(frames_in):
    frames_float = frames_in.astype(jnp.float32)
    centre = jnp.mean(frames_float, axis=-1, keepdims=True)
    shifted = frames_float - centre
    spread = jnp.mean(shifted * shifted, axis=-1, keepdims=True)
    inverse_spread = lax.rsqrt(spread + epsilon)
    return (frames_float, shifted * inverse_spread, inverse_spread)


def attend(packed, kept_mask):
    frames, places, row_width = packed.shape
    head_width = D // H
    pieces = packed.reshape(frames, places, 3, row_width // (3 * head_width), head_width)
    scores = jnp.einsum(
        "tphd,uphd->phtu", pieces[:, :, 0], pieces[:, :, 1], preferred_element_type=jnp.float32
    )
    scores = scores * head_width ** (-0.5)
    allowed = jnp.transpose(kept_mask)[:, None, None, :] > 0
    scores = jnp.where(allowed, scores, -1000000000.0)
    row_max = jnp.max(scores, axis=-1, keepdims=True)
    exponent = jnp.exp(scores - row_max)
    weights = (exponent / jnp.sum(exponent, axis=-1, keepdims=True)).astype(jnp.bfloat16)
    mixed_rows = jnp.einsum(
        "phtu,uphd->tphd", weights, pieces[:, :, 2], preferred_element_type=jnp.float32
    )
    mixed_rows = jnp.where(kept_mask[:, :, None, None] > 0, mixed_rows, 0.0)
    return mixed_rows.astype(jnp.bfloat16).reshape(frames, places, row_width // 3)


def project(rows_in, weight):
    leading = rows_in.shape[:-1]
    flat = jnp.dot(
        rows_in.reshape(-1, rows_in.shape[-1]), weight, preferred_element_type=jnp.float32
    )
    return flat.astype(jnp.bfloat16).reshape(leading + (weight.shape[1],))


def contract_rows(left, right):
    return lax.dot_general(
        left.reshape(-1, left.shape[-1]),
        right.reshape(-1, right.shape[-1]),
        (((0,), (0,)), ((), ())),
        preferred_element_type=jnp.float32,
    )


def back_project(cotangent, weight):
    leading = cotangent.shape[:-1]
    flat = lax.dot_general(
        cotangent.reshape(-1, cotangent.shape[-1]),
        weight,
        (((1,), (1,)), ((), ())),
        preferred_element_type=jnp.float32,
    )
    return flat.reshape(leading + (weight.shape[0],))


def body(frames_in, norm_gain, w_qkv, w_out, keep_runs, out_cotangent):
    frames_here, place_total, row_width = frames_in.shape
    places_here = place_total // lax.axis_size("tm")
    width_share = row_width // lax.axis_size("tensor")
    share_start = lax.axis_index("tensor") * width_share
    channels = w_qkv.shape[2]
    w_flat = w_qkv.reshape(row_width, 3 * channels)
    kept_mask = kept_table(keep_runs, lax.axis_index("tm") * places_here, places_here)
    frames_float, standard, inverse_spread = normalize(frames_in)
    normed = (standard * norm_gain).astype(jnp.bfloat16)
    packed = project(normed, w_flat)
    packed_places = lax.all_to_all(packed, "tm", split_axis=1, concat_axis=0, tiled=True)

    def attend_here(packed_arg):
        return attend(packed_arg, kept_mask)

    mixed_places, attend_back = jax.vjp(attend_here, packed_places)
    mixed_frames = lax.all_to_all(mixed_places, "tm", split_axis=0, concat_axis=1, tiled=True)
    branch = jnp.dot(mixed_frames.reshape(-1, channels), w_out, preferred_element_type=jnp.float32)
    branch = branch.reshape(frames_here, place_total, row_width)
    branch_share = lax.psum_scatter(
        branch.astype(jnp.bfloat16), "tensor", scatter_dimension=2, tiled=True
    ).astype(jnp.float32)
    residual_share = lax.dynamic_slice_in_dim(frames_float, share_start, width_share, 2)
    block_out = (residual_share + branch_share).astype(jnp.bfloat16)
    proj_part = contract_rows(mixed_frames, out_cotangent)
    grad_proj = lax.psum_scatter(proj_part, "tm", scatter_dimension=1, tiled=True).astype(
        jnp.bfloat16
    )
    mixed_cot = back_project(out_cotangent, w_out).astype(jnp.bfloat16)
    mixed_cot_places = lax.all_to_all(mixed_cot, "tm", split_axis=1, concat_axis=0, tiled=True)
    packed_cot_places = attend_back(mixed_cot_places)[0]
    gain_share = lax.dynamic_slice_in_dim(norm_gain, share_start, width_share, 0)
    standard_share = lax.dynamic_slice_in_dim(standard, share_start, width_share, 2)
    packed_cot = lax.all_to_all(packed_cot_places, "tm", split_axis=0, concat_axis=1, tiled=True)
    qkv_part = contract_rows(normed, packed_cot)
    normed_part = back_project(packed_cot, w_flat)
    whole_cot = lax.psum(normed_part.astype(jnp.bfloat16), "tensor").astype(jnp.float32)
    whole_cot = lax.optimization_barrier(whole_cot.astype(jnp.bfloat16)).astype(jnp.float32)
    scaled_whole = whole_cot * norm_gain
    mean_plain = jnp.mean(scaled_whole, axis=-1, keepdims=True)
    mean_cross = jnp.mean(scaled_whole * standard, axis=-1, keepdims=True)
    cot_share = lax.dynamic_slice_in_dim(whole_cot, share_start, width_share, 2)
    scaled_share = cot_share * gain_share
    through = inverse_spread * (scaled_share - mean_plain - standard_share * mean_cross)
    gain_part = jnp.sum(cot_share * standard_share, axis=(0, 1))
    cot_share_out = lax.dynamic_slice_in_dim(out_cotangent, share_start, width_share, 2).astype(
        jnp.float32
    )
    grad_in = (cot_share_out + through).astype(jnp.bfloat16)
    grad_qkv = lax.psum_scatter(
        qkv_part.reshape(row_width, 3, channels), "tm", scatter_dimension=0, tiled=True
    ).astype(jnp.bfloat16)
    grad_gain = lax.psum(gain_part, "tm")
    return (block_out, grad_in, grad_qkv, grad_proj, grad_gain)


def solution(mesh):
    in_specs = (
        P("tm", None, None),
        P(),
        P(None, None, "tensor"),
        P("tensor", None),
        P(),
        P("tm", None, None),
    )
    out_specs = (
        P("tm", None, "tensor"),
        P("tm", None, "tensor"),
        P("tm", None, "tensor"),
        P("tensor", "tm"),
        P("tensor"),
    )
    return jax.shard_map(body, mesh=mesh, in_specs=in_specs, out_specs=out_specs, check_vma=False)
```

profile of v0, /device:TPU:0, one launch (start us, length us, event | category | flops | bytes accessed | tf_op | source)
XLA Modules:
  0.0 338.7 jit_solution(6467486779215469923)
XLA Ops:
  8.0 2.2 fusion.29
  10.2 0.8 copy.115
  11.0 0.5 broadcast.97
  11.6 4.9 %reduce.4 = bf16[1024,192]{1,0:T(8,128)(2,1)} reduce(bf16[1024,1,192]{2,1,0:T(2,128)(2,1)S(1)} %bitcast.147, bf16[]{:T(256)} %broadcast.97), dimensions={1}, to_apply=%bitcast.110.reduce_sub_computation | reduce | bytes 786434
  16.5 2.4 reshape.160
  18.9 7.7 %all-to-all-start.2 = ((bf16[8,2,12288]{2,1,0:T(2,128)(2,1)}), bf16[8,2,12288]{2,1,0:T(2,128)(2,1)S(1)}, u32[]{:S(2)}, u32[]{:S(2)}) async-start(bf16[8,2,12288]{2,1,0:T(2,128)(2,1)} %reshape.160), calls=%async_computation.2 | async-start | bytes 786432 | tf_op jit(solution)/shard_map/all_to_all | solution.py:106
  27.0 0.6 multiply_reduce_fusion.1
  27.6 2.3 fusion.17
  29.9 6.2 %copy.106 = bf16[1,1024,576]{2,0,1:T(2,128)(2,1)} copy(bf16[1,1024,576]{1,2,0:T(8,128)(2,1)} %fusion.17) | data formatting | bytes 2359296 | tf_op jit(solution)/shard_map/reshape | solution.py:53
  36.1 11.0 %reduce.5 = bf16[1024,576]{1,0:T(8,128)(2,1)} reduce(bf16[1024,1,576]{2,1,0:T(2,128)(2,1)} %bitcast.141, bf16[]{:T(256)} %broadcast.97), dimensions={1}, to_apply=%bitcast.108.reduce_sub_computation | reduce | bytes 2359298
  47.1 4.4 %reshape.158 = bf16[8,2,36864]{2,1,0:T(2,128)(2,1)} reshape(bf16[1024,576]{1,0:T(8,128)(2,1)} %reduce.5) | data formatting | bytes 2359296
  51.5 17.1 %all-to-all-start = ((bf16[8,2,36864]{2,1,0:T(2,128)(2,1)}), bf16[8,2,36864]{2,1,0:T(2,128)(2,1)}, u32[]{:S(2)}, u32[]{:S(2)}) async-start(bf16[8,2,36864]{2,1,0:T(2,128)(2,1)} %reshape.158), calls=%async_computation | async-start | bytes 2359296 | tf_op jit(solution)/shard_map/all_to_all | solution.py:87
  69.0 2.4 reshape.161
  71.4 1.7 copy.116
  73.1 1.8 copy.143
  74.9 22.0 %all-to-all-done = bf16[8,2,36864]{2,1,0:T(2,128)(2,1)} async-done(((bf16[8,2,36864]{2,1,0:T(2,128)(2,1)}), bf16[8,2,36864]{2,1,0:T(2,128)(2,1)}, u32[]{:S(2)}, u32[]{:S(2)}) %all-to-all-start) | async-done | bytes 1179680 | tf_op jit(solution)/shard_map/all_to_all | solution.py:87
  96.9 6.5 %reshape.159 = bf16[1024,1,576]{2,1,0:T(2,128)(2,1)} reshape(bf16[8,2,36864]{2,1,0:T(2,128)(2,1)} %all-to-all-done) | data formatting | bytes 2359296
  103.4 6.0 %copy.107 = bf16[1,1024,576]{1,2,0:T(8,128)(2,1)} copy(bf16[1,1024,576]{2,0,1:T(2,128)(2,1)} %bitcast.142) | data formatting | bytes 2359296 | tf_op jit(solution)/shard_map/all_to_all | solution.py:87
  109.4 1.6 copy.142
  111.0 1.0 fusion.60
  112.0 1.6 copy.138
  113.6 2.7 copy.137
  116.3 2.4 copy.139
  118.7 2.0 fusion.62
  120.8 0.7 fusion.32
  121.5 0.8 multiply_divide_fusion
  122.5 1.6 fusion.39
  124.0 2.3 copy.113
  126.3 2.1 fusion.41
  128.4 3.5 %all-to-all-start.1 = ((bf16[8,128,192]{1,2,0:T(8,128)(2,1)}), bf16[8,128,192]{1,2,0:T(8,128)(2,1)S(1)}, u32[]{:S(2)}, u32[]{:S(2)}) async-start(bf16[8,128,192]{1,2,0:T(8,128)(2,1)} %bitcast.149), calls=%async_computation.1 | async-start | bytes 786432 | tf_op jit(solution)/shard_map/all_to_all | solution.py:93
  131.9 2.2 copy.118
  134.1 3.7 %convert_reduce_fusion.1 = (f32[128,3,8]{2,1,0:T(4,128)S(1)}, pred[128,3,8,8]{2,3,1,0:T(8,128)(4,1)S(1)}, f32[128,3,8]{2,1,0:T(4,128)S(1)}, bf16[128,3,8,8]{2,3,1,0:T(8,128)(2,1)S(1)}) fusion(f32[128,3,8,8]{2,3,1,0:T(8,128)} %copy-done.2, f32[128,3,8]{2,1,0:T(4,128)S(1)} %get-tuple-element.57, f32[128,3,8]{2,1,0:T(4,128)} %multiply_divide_fusion, ...), kind=kOutput, calls=%fused_computation.25 | convolution fusion | flops 3336192 | bytes 1007616 | tf_op jit(solution)/shard_map/transpose(jvp(phtu,uphd->tphd))/dot_general | solution.py:41
  137.9 1.0 fusion.58
  139.0 1.0 fusion.22
  140.2 0.7 fusion.21
  140.8 0.5 copy-done.12
  141.3 0.6 fusion.20
  141.9 2.0 pad_add_fusion
  143.9 4.0 %copy.121 = bf16[8,128,3,3,64]{1,4,3,2,0:T(8,128)(2,1)} copy(bf16[8,128,3,3,64]{4,0,3,1,2:T(8,128)(2,1)} %pad_add_fusion) | data formatting | bytes 2359296 | tf_op jit(solution)/shard_map/transpose(jvp())/add_any | solution.py:33
  147.9 6.0 %all-to-all-start.3 = ((bf16[8,128,576]{1,2,0:T(8,128)(2,1)}), bf16[8,128,576]{1,2,0:T(8,128)(2,1)}, u32[]{:S(2)}, u32[]{:S(2)}) async-start(bf16[8,128,576]{1,2,0:T(8,128)(2,1)} %bitcast.144), calls=%async_computation.3 | async-start | bytes 2359296 | tf_op jit(solution)/shard_map/all_to_all | solution.py:110
  153.9 3.0 fusion.23
  157.0 28.6 %all-to-all-done.3 = bf16[8,128,576]{1,2,0:T(8,128)(2,1)} async-done(((bf16[8,128,576]{1,2,0:T(8,128)(2,1)}), bf16[8,128,576]{1,2,0:T(8,128)(2,1)}, u32[]{:S(2)}, u32[]{:S(2)}) %all-to-all-start.3) | async-done | bytes 1179680 | tf_op jit(solution)/shard_map/all_to_all | solution.py:110
  185.6 3.9 %fusion.16 = bf16[1,1024,768]{2,1,0:T(8,128)(2,1)} fusion(bf16[768,576]{0,1:T(8,128)(2,1)S(1)} %bitcast.139, bf16[8,128,576]{1,2,0:T(8,128)(2,1)} %all-to-all-done.3), kind=kOutput, calls=%fused_computation.31 | convolution fusion | flops 906756096 | bytes 3637248 | tf_op jit(solution)/shard_map/dot_general | solution.py:67
  189.6 0.9 copy-done.10
  190.5 1.8 fusion.15
  192.2 8.5 %copy.130 = bf16[1,1024,768]{1,0,2:T(2,128)(2,1)} copy(bf16[1,1024,768]{2,1,0:T(8,128)(2,1)} %fusion.15) | data formatting | bytes 3145728
  200.7 3.7 %copy.158 = bf16[768,1,1024]{2,0,1:T(8,128)(2,1)} copy(bf16[768,1,1024]{2,1,0:T(2,128)(2,1)} %bitcast.140) | data formatting | bytes 3145728
  204.7 1.4 copy_bitcast_fusion.1
  206.1 3.3 fusion.4
  209.4 1.9 convert_element_type.92
  211.4 15.4 %reduce-scatter.12.cloned.1.call-done = f32[96,192]{1,0:T(8,128)} async-done(((f32[768,192]{1,0:T(8,128)}), f32[96,192]{1,0:T(8,128)}) %reduce-scatter.12.cloned.1.call-update) | async-done | bytes 73744
  226.8 1.6 copy.133
  228.4 3.5 %all-reduce.5.cloned.1.call-done = bf16[1,1024,768]{2,1,0:T(8,128)(2,1)} async-done(((bf16[1,1024,768]{2,1,0:T(8,128)(2,1)}), bf16[1,1024,768]{2,1,0:T(8,128)(2,1)}) %all-reduce.5.cloned.1.call-update) | async-done | bytes 1572880 | tf_op jit(solution)/shard_map/psum | solution.py:113
  232.0 1.8 convert_element_type.118
  233.9 1.2 multiply_reduce_fusion.2
  235.1 2.5 multiply_reduce_fusion.3
  237.6 0.9 copy.125
  238.5 21.8 %psum.15 = f32[192]{0:T(256)} all-reduce(f32[192]{0:T(256)S(1)} %get-tuple-element.46), channel_id=1, replica_groups=mesh['tm'=8,'tensor'=4] {'tm'}, use_global_device_ids=true, to_apply=%region_15.16 | all-reduce | flops 192 | bytes 1536 | tf_op jit(solution)/shard_map/psum | solution.py:129
  260.4 1.4 reshape_bitcast_fusion
  261.8 1.1 copy.131
  262.9 1.8 add_convert_fusion.1
  264.7 0.9 copy.124
  265.6 64.1 %reduce-scatter.8.cloned.1.call-done = f32[96,3,192]{2,0,1:T(8,128)} async-done(((f32[768,3,192]{2,0,1:T(8,128)}), f32[96,3,192]{2,0,1:T(8,128)}) %reduce-scatter.8.cloned.1.call-update) | async-done | bytes 221200 | tf_op jit(solution)/shard_map/reduce_scatter | solution.py:126
  329.7 1.6 convert_element_type.120
  (53 shorter events, 1.8 us)
Async XLA Ops:
  8.0 19.6 %copy-start = (bf16[768,3,192]{0,2,1:T(8,128)(2,1)S(1)}, bf16[768,3,192]{0,2,1:T(8,128)(2,1)}, u32[]{:S(2)}) copy-start(bf16[768,3,192]{0,2,1:T(8,128)(2,1)} %param.8) | copy-start | bytes 2654212
  11.6 15.1 %copy-start.1 = (bf16[1,1024,768]{2,1,0:T(8,128)(2,1)S(1)}, bf16[1,1024,768]{2,1,0:T(8,128)(2,1)}, u32[]{:S(2)}) copy-start(bf16[1,1024,768]{2,1,0:T(8,128)(2,1)} %param.6) | copy-start | bytes 4718596
  18.9 32.6 %all-to-all-start.2 = ((bf16[8,2,12288]{2,1,0:T(2,128)(2,1)}), bf16[8,2,12288]{2,1,0:T(2,128)(2,1)S(1)}, u32[]{:S(2)}, u32[]{:S(2)}) async-start(bf16[8,2,12288]{2,1,0:T(2,128)(2,1)} %reshape.160), calls=%async_computation.2 | async-start | bytes 786432 | tf_op jit(solution)/shard_map/all_to_all | solution.py:106
  26.7 0.9 copy-start.14
  51.5 17.2 %copy-start.13 = (s32[8,16,2]{1,2,0:T(2,128)S(1)}, s32[8,16,2]{1,2,0:T(2,128)}, u32[]{:S(2)}) copy-start(s32[8,16,2]{1,2,0:T(2,128)} %param.10) | copy-start | bytes 3076
  51.5 17.5 %copy-start.8 = (bf16[8,2,12288]{2,1,0:T(2,128)(2,1)}, bf16[8,2,12288]{2,1,0:T(2,128)(2,1)S(1)}, u32[]{:S(2)}) copy-start(bf16[8,2,12288]{2,1,0:T(2,128)(2,1)S(1)} %all-to-all-done.2) | copy-start | bytes 1179652
  51.5 45.4 %all-to-all-start = ((bf16[8,2,36864]{2,1,0:T(2,128)(2,1)}), bf16[8,2,36864]{2,1,0:T(2,128)(2,1)}, u32[]{:S(2)}, u32[]{:S(2)}) async-start(bf16[8,2,36864]{2,1,0:T(2,128)(2,1)} %reshape.158), calls=%async_computation | async-start | bytes 2359296 | tf_op jit(solution)/shard_map/all_to_all | solution.py:87
  113.6 7.1 %copy-start.5 = (bf16[8,128,1,3,64]{4,0,3,1,2:T(8,128)(2,1)}, bf16[8,128,1,3,64]{4,0,3,1,2:T(8,128)(2,1)S(1)}, u32[]{:S(2)}) copy-start(bf16[8,128,1,3,64]{4,0,3,1,2:T(8,128)(2,1)S(1)} %copy.138) | copy-start | bytes 1179652
  120.7 1.5 copy-start.2
  120.7 1.7 copy-start.11
  122.4 3.9 %copy-start.9 = (bf16[24,8,8,128]{3,2,1,0:T(8,128)(2,1)S(1)}, bf16[24,8,8,128]{3,2,1,0:T(8,128)(2,1)}, u32[]{:S(2)}) copy-start(bf16[24,8,8,128]{3,2,1,0:T(8,128)(2,1)} %copy.143) | copy-start | bytes 1179652
  128.4 19.5 %all-to-all-start.1 = ((bf16[8,128,192]{1,2,0:T(8,128)(2,1)}), bf16[8,128,192]{1,2,0:T(8,128)(2,1)S(1)}, u32[]{:S(2)}, u32[]{:S(2)}) async-start(bf16[8,128,192]{1,2,0:T(8,128)(2,1)} %bitcast.149), calls=%async_computation.1 | async-start | bytes 786432 | tf_op jit(solution)/shard_map/all_to_all | solution.py:93
  134.1 3.8 %copy-start.3 = (f32[128,3,8,8]{2,3,1,0:T(8,128)S(1)}, f32[128,3,8,8]{2,3,1,0:T(8,128)}, u32[]{:S(2)}) copy-start(f32[128,3,8,8]{2,3,1,0:T(8,128)} %copy-done.2) | copy-start | bytes 294916
  137.9 1.1 copy-start.7
  139.0 1.1 copy-start.6
  140.2 1.1 copy-start.12
  147.9 37.7 %all-to-all-start.3 = ((bf16[8,128,576]{1,2,0:T(8,128)(2,1)}), bf16[8,128,576]{1,2,0:T(8,128)(2,1)}, u32[]{:S(2)}, u32[]{:S(2)}) async-start(bf16[8,128,576]{1,2,0:T(8,128)(2,1)} %bitcast.144), calls=%async_computation.3 | async-start | bytes 2359296 | tf_op jit(solution)/shard_map/all_to_all | solution.py:110
  153.9 72.9 %reduce-scatter.12.cloned.1.call-start = ((), (), s32[]{:S(2)}) async-start(), calls=%async_computation.10 | async-start | bytes 884736
  157.0 75.0 %all-reduce.5.cloned.1.call-start = ((), (), s32[]{:S(2)}) async-start(), calls=%async_computation.7 | async-start | bytes 3145728 | tf_op jit(solution)/shard_map/psum | solution.py:113
  189.5 1.0 copy-start.10
  189.5 70.8 %reduce-scatter.10.cloned.1.call-start = ((), (), s32[]{:S(2)}) async-start(), calls=%async_computation.9 | async-start | bytes 1966080
  204.4 125.2 %reduce-scatter.8.cloned.1.call-start = ((), (), s32[]{:S(2)}) async-start(), calls=%async_computation.8 | async-start | bytes 2654208 | tf_op jit(solution)/shard_map/reduce_scatter | solution.py:126
  232.0 2.0 copy-start.4
Sparse Core Ops, SparseCore 0:
  158.0 68.7 reduce-scatter.11
  229.4 27.0 reduce-scatter.9
  260.0 69.6 reduce-scatter.7
Sparse Core Ops, SparseCore 1:
  189.6 42.3 all-reduce.4
where the time goes:
time: 345 us; the launch traced here: 339 us
  waiting for transfers between devices  134 us (39%)
  local copies, waits for them, and re-layouts  72.4 us (21%)
  starting transfers between devices  34.6 us (10%)
  other arithmetic  34.4 us (10%)
  matrix products  25.9 us (8%)
  blocking collectives  21.8 us (6%)
  between operations  15.8 us (5%)
    reduce_scatter x1, waiting for transfers between devices, body(): lax.psum_scatter(qkv_part.reshape(row_width, 3, channels), 'tm', scatter_...  64.1 us
    unnamed x47, local copies, waits for them, and re-layouts  46.5 us
    all_to_all x1, waiting for transfers between devices, body(): lax.all_to_all(packed_cot_places, 'tm', split_axis=0, concat_axis=1, tile...  28.6 us
    all_to_all x1, waiting for transfers between devices, body(): lax.all_to_all(packed, 'tm', split_axis=1, concat_axis=0, tiled=True)  22 us
    psum x1, blocking collectives, body(): grad_gain = lax.psum(gain_part, 'tm')  21.8 us
    all_to_all x1, starting transfers between devices, body(): lax.all_to_all(packed, 'tm', split_axis=1, concat_axis=0, tiled=True)  17.1 us
    unnamed x2, other arithmetic  16 us
    unnamed x6, waiting for transfers between devices  15.5 us
  transfers between devices with their start and end apart: 8, of which 5 were waited for; matrix products, arithmetic and copies ran while one was open for 26% of the time, Pallas kernels for 0%

commit v1 on v0

--- a/solution.py
+++ b/solution.py
@@ -84,7 +84,19 @@
     frames_float, standard, inverse_spread = normalize(frames_in)
     normed = (standard * norm_gain).astype(jnp.bfloat16)
     packed = project(normed, w_flat)
-    packed_places = lax.all_to_all(packed, "tm", split_axis=1, concat_axis=0, tiled=True)
+    ways, here = (lax.axis_size("tm"), lax.axis_index("tm"))
+    width = packed.shape[1] // ways
+    dims = list(packed.shape)
+    dims[1] = width
+    height = dims[0]
+    dims[0] = height * ways
+    full = jnp.zeros(dims, packed.dtype)
+    for mask in range(ways):
+        part = lax.dynamic_slice_in_dim(packed, (here ^ mask) * width, width, axis=1)
+        if mask:
+            part = lax.ppermute(part, "tm", [(d, d ^ mask) for d in range(ways)])
+        full = lax.dynamic_update_slice_in_dim(full, part, (here ^ mask) * height, axis=0)
+    packed_places = full
 
     def attend_here(packed_arg):
         return attend(packed_arg, kept_mask)

time: 345 us -> 305 us (0.88); the launches traced: 339 us -> 303 us
  waiting for transfers between devices: 134 us -> 121 us
  local copies, waits for them, and re-layouts: 72.4 us -> 60.1 us
  other arithmetic: 34.4 us -> 23.3 us
    all_to_all x1 -> x0, waiting for transfers between devices: 22 us -> none  [body(): lax.all_to_all(packed, 'tm', split_axis=1, concat_axis=0, tiled=True)]
    all_to_all x1 -> x0, starting transfers between devices: 17.1 us -> none  [body(): lax.all_to_all(packed, 'tm', split_axis=1, concat_axis=0, tiled=True)]
    ppermute x0 -> x7, starting transfers between devices: none -> 16.3 us  [body(): part = lax.ppermute(part, 'tm', [(d, d ^ mask) for d in range(ways)])]
    unnamed x47 -> x50, local copies, waits for them, and re-layouts: 46.5 us -> 33.8 us
    unnamed x2 -> x1, other arithmetic: 16 us -> 4.94 us
    dynamic_update_slice x0 -> x8, local copies, waits for them, and re-layouts: none -> 10.8 us  [body(): lax.dynamic_update_slice_in_dim(full, part, (here ^ mask) * height, axis=0)]
    ppermute x0 -> x7, waiting for transfers between devices: none -> 10.2 us  [body(): part = lax.ppermute(part, 'tm', [(d, d ^ mask) for d in range(ways)])]
    reshape x1 -> x0, local copies, waits for them, and re-layouts: 6.18 us -> none  [project(): return flat.astype(jnp.bfloat16).reshape(leading + (weight.shape[1],))]
  transfers between devices with their start and end apart: 8 -> 14, of which waited for: 5 -> 6; matrix products, arithmetic and copies ran while one was open for 26% -> 28% of each run, Pallas kernels for 0% -> 0%
where the time goes in v1:
time: 305 us; the launch traced here: 303 us
  waiting for transfers between devices  121 us (40%)
  local copies, waits for them, and re-layouts  60.1 us (20%)
  starting transfers between devices  34.3 us (11%)
  matrix products  26.5 us (9%)
  other arithmetic  23.3 us (8%)
  blocking collectives  21.7 us (7%)
  between operations  15.6 us (5%)
    reduce_scatter x1, waiting for transfers between devices, body(): lax.psum_scatter(qkv_part.reshape(row_width, 3, channels), 'tm', scatter_...  63.9 us
    unnamed x50, local copies, waits for them, and re-layouts  33.8 us
    all_to_all x1, waiting for transfers between devices, body(): lax.all_to_all(packed_cot_places, 'tm', split_axis=0, concat_axis=1, tile...  28.7 us
    psum x1, blocking collectives, body(): grad_gain = lax.psum(gain_part, 'tm')  21.7 us
    ppermute x7, starting transfers between devices, body(): part = lax.ppermute(part, 'tm', [(d, d ^ mask) for d in range(ways)])  16.3 us
    unnamed x6, waiting for transfers between devices  14.8 us
    dynamic_update_slice x8, local copies, waits for them, and re-layouts, body(): lax.dynamic_update_slice_in_dim(full, part, (here ^ mask) * height, axis=0)  10.8 us
    ppermute x7, waiting for transfers between devices, body(): part = lax.ppermute(part, 'tm', [(d, d ^ mask) for d in range(ways)])  10.2 us
  transfers between devices with their start and end apart: 14, of which 6 were waited for; matrix products, arithmetic and copies ran while one was open for 28% of the time, Pallas kernels for 0%

profile of v1, /device:TPU:0, one launch (start us, length us, event | category | flops | bytes accessed | tf_op | source)
XLA Modules:
  0.0 303.0 jit_solution(10116686517193640591)
XLA Ops:
  8.0 2.2 fusion.26
  10.2 0.8 copy.91
  11.6 4.9 %reduce.4 = bf16[1024,192]{1,0:T(8,128)(2,1)} reduce(bf16[1024,1,192]{2,1,0:T(2,128)(2,1)S(1)} %bitcast.148, bf16[]{:T(256)} %broadcast.97), dimensions={1}, to_apply=%bitcast.115.reduce_sub_computation | reduce | bytes 786434
  16.5 2.4 reshape.159
  18.9 7.3 %all-to-all-start.1 = ((bf16[8,2,12288]{2,1,0:T(2,128)(2,1)}), bf16[8,2,12288]{2,1,0:T(2,128)(2,1)}, u32[]{:S(2)}, u32[]{:S(2)}) async-start(bf16[8,2,12288]{2,1,0:T(2,128)(2,1)} %reshape.159), calls=%async_computation.1 | async-start | bytes 786432 | tf_op jit(solution)/shard_map/all_to_all | solution.py:118
  27.2 1.3 fusion.12
  28.5 1.0 copy-done.14
  29.8 4.8 %collective-permute-start.6 = (bf16[1,128,576]{1,2,0:T(8,128)(2,1)S(1)}, bf16[1,128,576]{1,2,0:T(8,128)(2,1)}, u32[]{:S(2)}, u32[]{:S(2)}) collective-permute-start(bf16[1,128,576]{1,2,0:T(8,128)(2,1)S(1)} %get-tuple-element.48), channel_id=1, source_target_pairs={{0,28},{4,24},{8,20},{12,16},{16,12},{20,8},{24,4},{28,0},{1,29},{... | collective-permute-start | bytes 442376 | tf_op jit(solution)/shard_map/ppermute | solution.py:97
  35.7 3.3 %collective-permute-start.1 = (bf16[1,128,576]{1,2,0:T(8,128)(2,1)S(1)}, bf16[1,128,576]{1,2,0:T(8,128)(2,1)}, u32[]{:S(2)}, u32[]{:S(2)}) collective-permute-start(bf16[1,128,576]{1,2,0:T(8,128)(2,1)S(1)} %get-tuple-element.53), channel_id=1, source_target_pairs={{0,8},{4,12},{8,0},{12,4},{16,24},{20,28},{24,16},{28,20},{1,9},{5... | collective-permute-start | bytes 442376 | tf_op jit(solution)/shard_map/ppermute | solution.py:97
  38.9 1.5 collective-permute-start
  40.6 1.2 broadcast_in_dim.63
  41.8 1.6 bitcast_dynamic-update-slice_fusion
  44.2 3.4 %collective-permute-start.2 = (bf16[1,128,576]{1,2,0:T(8,128)(2,1)S(1)}, bf16[1,128,576]{1,2,0:T(8,128)(2,1)S(1)}, u32[]{:S(2)}, u32[]{:S(2)}) collective-permute-start(bf16[1,128,576]{1,2,0:T(8,128)(2,1)S(1)} %get-tuple-element.52), channel_id=1, source_target_pairs={{0,12},{4,8},{8,4},{12,0},{16,28},{20,24},{24,20},{28,16},{1,13},{... | collective-permute-start | bytes 442376 | tf_op jit(solution)/shard_map/ppermute | solution.py:97
  47.6 1.6 constant_dynamic-update-slice_fusion.6
  49.2 2.3 collective-permute-start.3
  51.5 1.6 constant_dynamic-update-slice_fusion.5
  53.7 9.5 %collective-permute-done.3 = bf16[1,128,576]{1,2,0:T(8,128)(2,1)S(1)} collective-permute-done((bf16[1,128,576]{1,2,0:T(8,128)(2,1)S(1)}, bf16[1,128,576]{1,2,0:T(8,128)(2,1)S(1)}, u32[]{:S(2)}, u32[]{:S(2)}) %collective-permute-start.3) | collective-permute-done | bytes 147488 | tf_op jit(solution)/shard_map/ppermute | solution.py:97
  63.9 1.6 constant_dynamic-update-slice_fusion.2
  65.4 1.6 constant_dynamic-update-slice_fusion.1
  67.0 1.6 constant_dynamic-update-slice_fusion
  68.6 2.3 fusion.57
  70.9 1.4 copy.114
  72.3 2.5 copy.115
  74.8 2.0 fusion.59
  76.9 1.1 copy-done.2
  78.7 1.3 copy.113
  80.0 3.2 %fusion.36 = bf16[128,3,64,8]{2,3,1,0:T(8,128)(2,1)} fusion(bf16[8,128,1,3,64]{4,0,3,1,2:T(8,128)(2,1)} %copy.113, f32[128,3,8,8]{2,3,1,0:T(8,128)} %copy-done.2, f32[128,3,8]{2,1,0:T(4,128)S(1)} %fusion.29, f32[128,3,8]{2,1,0:T(4,128)S(1)} %get-tuple-element.59), kind=kOutput, calls=%fused_computation.55 | convolution fusion | flops 3219456 | bytes 909312 | tf_op jit(solution)/shard_map/jvp(phtu,uphd->tphd)/dot_general | solution.py:41
  83.2 2.3 copy.89
  86.2 2.3 reshape.160
  88.6 1.7 copy.92
  90.4 1.1 copy.118
  91.4 2.0 fusion.38
  93.4 4.3 %all-to-all-start = ((bf16[8,128,192]{1,2,0:T(8,128)(2,1)}), bf16[8,128,192]{1,2,0:T(8,128)(2,1)S(1)}, u32[]{:S(2)}, u32[]{:S(2)}) async-start(bf16[8,128,192]{1,2,0:T(8,128)(2,1)} %bitcast.18), calls=%async_computation | async-start | bytes 786432 | tf_op jit(solution)/shard_map/all_to_all | solution.py:105
  97.7 1.2 copy.94
  99.0 3.7 %convert_reduce_fusion.1 = (f32[128,3,8]{2,1,0:T(4,128)S(1)}, pred[128,3,8,8]{2,3,1,0:T(8,128)(4,1)S(1)}, f32[128,3,8]{2,1,0:T(4,128)S(1)}, bf16[128,3,8,8]{2,3,1,0:T(8,128)(2,1)S(1)}) fusion(f32[128,3,8,8]{2,3,1,0:T(8,128)} %copy-done.2, f32[128,3,8]{2,1,0:T(4,128)S(1)} %copy-done.11, f32[128,3,8]{2,1,0:T(4,128)} %multiply_divide_fusion, ...), kind=kOutput, calls=%fused_computation.25 | convolution fusion | flops 3336192 | bytes 1007616 | tf_op jit(solution)/shard_map/transpose(jvp(phtu,uphd->tphd))/dot_general | solution.py:41
  102.8 1.0 fusion.55
  103.9 1.0 fusion.19
  106.8 2.0 pad_add_fusion
  108.8 4.0 %copy.97 = bf16[8,128,3,3,64]{1,4,3,2,0:T(8,128)(2,1)} copy(bf16[8,128,3,3,64]{4,0,3,1,2:T(8,128)(2,1)} %pad_add_fusion) | data formatting | bytes 2359296 | tf_op jit(solution)/shard_map/transpose(jvp())/add_any | solution.py:33
  112.8 6.0 %all-to-all-start.2 = ((bf16[8,128,576]{1,2,0:T(8,128)(2,1)}), bf16[8,128,576]{1,2,0:T(8,128)(2,1)}, u32[]{:S(2)}, u32[]{:S(2)}) async-start(bf16[8,128,576]{1,2,0:T(8,128)(2,1)} %bitcast.147), calls=%async_computation.2 | async-start | bytes 2359296 | tf_op jit(solution)/shard_map/all_to_all | solution.py:122
  118.8 3.0 fusion.20
  121.9 28.7 %all-to-all-done.2 = bf16[8,128,576]{1,2,0:T(8,128)(2,1)} async-done(((bf16[8,128,576]{1,2,0:T(8,128)(2,1)}), bf16[8,128,576]{1,2,0:T(8,128)(2,1)}, u32[]{:S(2)}, u32[]{:S(2)}) %all-to-all-start.2) | async-done | bytes 1179680 | tf_op jit(solution)/shard_map/all_to_all | solution.py:122
  150.7 3.9 %fusion.16 = bf16[1,1024,768]{2,1,0:T(8,128)(2,1)} fusion(bf16[768,576]{0,1:T(8,128)(2,1)S(1)} %bitcast.144, bf16[8,128,576]{1,2,0:T(8,128)(2,1)} %all-to-all-done.2), kind=kOutput, calls=%fused_computation.31 | convolution fusion | flops 906756096 | bytes 3637248 | tf_op jit(solution)/shard_map/dot_general | solution.py:67
  154.6 0.9 copy-done.13
  155.5 1.8 fusion.15
  157.3 8.5 %copy.106 = bf16[1,1024,768]{1,0,2:T(2,128)(2,1)} copy(bf16[1,1024,768]{2,1,0:T(8,128)(2,1)} %fusion.15) | data formatting | bytes 3145728
  165.8 3.7 %copy.133 = bf16[768,1,1024]{2,0,1:T(8,128)(2,1)} copy(bf16[768,1,1024]{2,1,0:T(2,128)(2,1)} %bitcast.145) | data formatting | bytes 3145728
  169.8 1.5 copy_bitcast_fusion.1
  171.3 3.3 %fusion.4 = f32[768,3,192]{2,0,1:T(8,128)} fusion(bf16[3,192,1024]{2,1,0:T(8,128)(2,1)S(1)} %bitcast.152, f32[768]{0:T(1024)S(1)} %copy-done.17, bf16[1,1024,768]{2,1,0:T(8,128)(2,1)S(1)} %copy-done.1, f32[1024]{0:T(1024)S(1)} %add_rsqrt_fusion, f32[1024]{0:T(1024)S(1)} %broadcast_multiply_fusion.2), kind=kOutput, calls=%fused_computation.16 | convolution fusion | flops 909901824 | bytes 4533248 | tf_op jit(solution)/shard_map/dot_general | solution.py:57
  174.6 1.9 convert_element_type.92
  176.6 14.7 %reduce-scatter.12.cloned.1.call-done = f32[96,192]{1,0:T(8,128)} async-done(((f32[768,192]{1,0:T(8,128)}), f32[96,192]{1,0:T(8,128)}) %reduce-scatter.12.cloned.1.call-update) | async-done | bytes 73744
  191.3 1.6 copy.109
  192.9 3.7 %all-reduce.5.cloned.1.call-done = bf16[1,1024,768]{2,1,0:T(8,128)(2,1)} async-done(((bf16[1,1024,768]{2,1,0:T(8,128)(2,1)}), bf16[1,1024,768]{2,1,0:T(8,128)(2,1)}) %all-reduce.5.cloned.1.call-update) | async-done | bytes 1572880 | tf_op jit(solution)/shard_map/psum | solution.py:125
  196.6 1.8 convert_element_type.118
  198.7 1.2 multiply_reduce_fusion.2
  199.9 2.5 multiply_reduce_fusion.3
  202.4 0.9 copy.101
  203.3 21.7 %psum.15 = f32[192]{0:T(256)} all-reduce(f32[192]{0:T(256)S(1)} %get-tuple-element.41), channel_id=1, replica_groups=mesh['tm'=8,'tensor'=4] {'tm'}, use_global_device_ids=true, to_apply=%region_15.16 | all-reduce | flops 192 | bytes 1536 | tf_op jit(solution)/shard_map/psum | solution.py:141
  225.0 1.4 reshape_bitcast_fusion
  226.4 1.1 copy.107
  227.6 1.8 add_convert_fusion.1
  229.3 0.9 copy.100
  230.3 63.9 %reduce-scatter.8.cloned.1.call-done = f32[96,3,192]{2,0,1:T(8,128)} async-done(((f32[768,3,192]{2,0,1:T(8,128)}), f32[96,3,192]{2,0,1:T(8,128)}) %reduce-scatter.8.cloned.1.call-update) | async-done | bytes 221200 | tf_op jit(solution)/shard_map/reduce_scatter | solution.py:138
  294.2 1.6 convert_element_type.120
  (75 shorter events, 9.6 us)
Async XLA Ops:
  8.0 19.2 %copy-start = (bf16[768,3,192]{0,2,1:T(8,128)(2,1)S(1)}, bf16[768,3,192]{0,2,1:T(8,128)(2,1)}, u32[]{:S(2)}) copy-start(bf16[768,3,192]{0,2,1:T(8,128)(2,1)} %param.8) | copy-start | bytes 2654212
  11.6 14.7 %copy-start.1 = (bf16[1,1024,768]{2,1,0:T(8,128)(2,1)S(1)}, bf16[1,1024,768]{2,1,0:T(8,128)(2,1)}, u32[]{:S(2)}) copy-start(bf16[1,1024,768]{2,1,0:T(8,128)(2,1)} %param.6) | copy-start | bytes 4718596
  18.9 67.3 %all-to-all-start.1 = ((bf16[8,2,12288]{2,1,0:T(2,128)(2,1)}), bf16[8,2,12288]{2,1,0:T(2,128)(2,1)}, u32[]{:S(2)}, u32[]{:S(2)}) async-start(bf16[8,2,12288]{2,1,0:T(2,128)(2,1)} %reshape.159), calls=%async_computation.1 | async-start | bytes 786432 | tf_op jit(solution)/shard_map/all_to_all | solution.py:118
  26.2 1.0 copy-start.17
  28.5 1.0 copy-start.14
  29.5 10.9 %copy-start.16 = (s32[8,16,2]{1,2,0:T(2,128)S(1)}, s32[8,16,2]{1,2,0:T(2,128)}, u32[]{:S(2)}) copy-start(s32[8,16,2]{1,2,0:T(2,128)} %param.10) | copy-start | bytes 3076
  29.8 37.2 %collective-permute-start.6 = (bf16[1,128,576]{1,2,0:T(8,128)(2,1)S(1)}, bf16[1,128,576]{1,2,0:T(8,128)(2,1)}, u32[]{:S(2)}, u32[]{:S(2)}) collective-permute-start(bf16[1,128,576]{1,2,0:T(8,128)(2,1)S(1)} %get-tuple-element.48), channel_id=1, source_target_pairs={{0,28},{4,24},{8,20},{12,16},{16,12},{20,8},{24,4},{28,0},{1,29},{... | collective-permute-start | bytes 442376 | tf_op jit(solution)/shard_map/ppermute | solution.py:97
  34.6 30.9 %collective-permute-start.5 = (bf16[1,128,576]{1,2,0:T(8,128)(2,1)S(1)}, bf16[1,128,576]{1,2,0:T(8,128)(2,1)}, u32[]{:S(2)}, u32[]{:S(2)}) collective-permute-start(bf16[1,128,576]{1,2,0:T(8,128)(2,1)S(1)} %get-tuple-element.49), channel_id=1, source_target_pairs={{0,24},{4,28},{8,16},{12,20},{16,8},{20,12},{24,0},{28,4},{1,25},{... | collective-permute-start | bytes 442376 | tf_op jit(solution)/shard_map/ppermute | solution.py:97
  35.1 28.7 %collective-permute-start.4 = (bf16[1,128,576]{1,2,0:T(8,128)(2,1)S(1)}, bf16[1,128,576]{1,2,0:T(8,128)(2,1)}, u32[]{:S(2)}, u32[]{:S(2)}) collective-permute-start(bf16[1,128,576]{1,2,0:T(8,128)(2,1)S(1)} %get-tuple-element.50), channel_id=1, source_target_pairs={{0,20},{4,16},{8,28},{12,24},{16,4},{20,0},{24,12},{28,8},{1,21},{... | collective-permute-start | bytes 442376 | tf_op jit(solution)/shard_map/ppermute | solution.py:97
  35.7 13.5 %collective-permute-start.1 = (bf16[1,128,576]{1,2,0:T(8,128)(2,1)S(1)}, bf16[1,128,576]{1,2,0:T(8,128)(2,1)}, u32[]{:S(2)}, u32[]{:S(2)}) collective-permute-start(bf16[1,128,576]{1,2,0:T(8,128)(2,1)S(1)} %get-tuple-element.53), channel_id=1, source_target_pairs={{0,8},{4,12},{8,0},{12,4},{16,24},{20,28},{24,16},{28,20},{1,9},{5... | collective-permute-start | bytes 442376 | tf_op jit(solution)/shard_map/ppermute | solution.py:97
  38.9 5.3 %collective-permute-start = (bf16[1,128,576]{1,2,0:T(8,128)(2,1)S(1)}, bf16[1,128,576]{1,2,0:T(8,128)(2,1)}, u32[]{:S(2)}, u32[]{:S(2)}) collective-permute-start(bf16[1,128,576]{1,2,0:T(8,128)(2,1)S(1)} %get-tuple-element.54), channel_id=1, source_target_pairs={{0,4},{4,0},{8,12},{12,8},{16,20},{20,16},{24,28},{28,24},{1,5},{5... | collective-permute-start | bytes 442376 | tf_op jit(solution)/shard_map/ppermute | solution.py:97
  44.2 8.8 %collective-permute-start.2 = (bf16[1,128,576]{1,2,0:T(8,128)(2,1)S(1)}, bf16[1,128,576]{1,2,0:T(8,128)(2,1)S(1)}, u32[]{:S(2)}, u32[]{:S(2)}) collective-permute-start(bf16[1,128,576]{1,2,0:T(8,128)(2,1)S(1)} %get-tuple-element.52), channel_id=1, source_target_pairs={{0,12},{4,8},{8,4},{12,0},{16,28},{20,24},{24,20},{28,16},{1,13},{... | collective-permute-start | bytes 442376 | tf_op jit(solution)/shard_map/ppermute | solution.py:97
  49.2 14.0 %collective-permute-start.3 = (bf16[1,128,576]{1,2,0:T(8,128)(2,1)S(1)}, bf16[1,128,576]{1,2,0:T(8,128)(2,1)S(1)}, u32[]{:S(2)}, u32[]{:S(2)}) collective-permute-start(bf16[1,128,576]{1,2,0:T(8,128)(2,1)S(1)} %get-tuple-element.51), channel_id=1, source_target_pairs={{0,16},{4,20},{8,24},{12,28},{16,0},{20,4},{24,8},{28,12},{1,17},{... | collective-permute-start | bytes 442376 | tf_op jit(solution)/shard_map/ppermute | solution.py:97
  72.3 4.5 %copy-start.5 = (bf16[8,128,1,3,64]{4,0,3,1,2:T(8,128)(2,1)}, bf16[8,128,1,3,64]{4,0,3,1,2:T(8,128)(2,1)S(1)}, u32[]{:S(2)}) copy-start(bf16[8,128,1,3,64]{4,0,3,1,2:T(8,128)(2,1)S(1)} %copy.114) | copy-start | bytes 1179652
  76.8 1.2 copy-start.2
  76.8 3.2 %copy-start.10 = (f32[128,3,8]{2,1,0:T(4,128)}, f32[128,3,8]{2,1,0:T(4,128)S(1)}, u32[]{:S(2)}) copy-start(f32[128,3,8]{2,1,0:T(4,128)S(1)} %get-tuple-element.59) | copy-start | bytes 36868
  76.8 1.9 copy-start.12
  78.7 6.8 %copy-start.8 = (f32[128,3,8]{2,1,0:T(4,128)}, f32[128,3,8]{2,1,0:T(4,128)S(1)}, u32[]{:S(2)}) copy-start(f32[128,3,8]{2,1,0:T(4,128)S(1)} %fusion.29) | copy-start | bytes 36868
  91.4 7.6 %copy-start.11 = (f32[128,3,8]{2,1,0:T(4,128)S(1)}, f32[128,3,8]{2,1,0:T(4,128)}, u32[]{:S(2)}) copy-start(f32[128,3,8]{2,1,0:T(4,128)} %copy-done.10) | copy-start | bytes 36868
  93.4 19.3 %all-to-all-start = ((bf16[8,128,192]{1,2,0:T(8,128)(2,1)}), bf16[8,128,192]{1,2,0:T(8,128)(2,1)S(1)}, u32[]{:S(2)}, u32[]{:S(2)}) async-start(bf16[8,128,192]{1,2,0:T(8,128)(2,1)} %bitcast.18), calls=%async_computation | async-start | bytes 786432 | tf_op jit(solution)/shard_map/all_to_all | solution.py:105
  99.0 3.8 %copy-start.3 = (f32[128,3,8,8]{2,3,1,0:T(8,128)S(1)}, f32[128,3,8,8]{2,3,1,0:T(8,128)}, u32[]{:S(2)}) copy-start(f32[128,3,8,8]{2,3,1,0:T(8,128)} %copy-done.2) | copy-start | bytes 294916
  99.0 3.8 %copy-start.9 = (f32[128,3,8]{2,1,0:T(4,128)S(1)}, f32[128,3,8]{2,1,0:T(4,128)}, u32[]{:S(2)}) copy-start(f32[128,3,8]{2,1,0:T(4,128)} %copy-done.8) | copy-start | bytes 36868
  102.8 1.1 copy-start.7
  103.9 1.1 copy-start.6
  105.1 1.1 copy-start.15
  112.8 37.9 %all-to-all-start.2 = ((bf16[8,128,576]{1,2,0:T(8,128)(2,1)}), bf16[8,128,576]{1,2,0:T(8,128)(2,1)}, u32[]{:S(2)}, u32[]{:S(2)}) async-start(bf16[8,128,576]{1,2,0:T(8,128)(2,1)} %bitcast.147), calls=%async_computation.2 | async-start | bytes 2359296 | tf_op jit(solution)/shard_map/all_to_all | solution.py:122
  118.8 72.5 %reduce-scatter.12.cloned.1.call-start = ((), (), s32[]{:S(2)}) async-start(), calls=%async_computation.9 | async-start | bytes 884736
  121.9 74.8 %all-reduce.5.cloned.1.call-start = ((), (), s32[]{:S(2)}) async-start(), calls=%async_computation.6 | async-start | bytes 3145728 | tf_op jit(solution)/shard_map/psum | solution.py:125
  154.6 1.0 copy-start.13
  154.6 70.4 %reduce-scatter.10.cloned.1.call-start = ((), (), s32[]{:S(2)}) async-start(), calls=%async_computation.8 | async-start | bytes 1966080
  169.5 124.7 %reduce-scatter.8.cloned.1.call-start = ((), (), s32[]{:S(2)}) async-start(), calls=%async_computation.7 | async-start | bytes 2654208 | tf_op jit(solution)/shard_map/reduce_scatter | solution.py:138
  196.6 2.1 copy-start.4
Sparse Core Ops, SparseCore 0:
  122.9 68.3 reduce-scatter.11
  193.8 27.0 reduce-scatter.9
  224.4 69.7 reduce-scatter.7
Sparse Core Ops, SparseCore 1:
  154.7 41.9 all-reduce.4
